TPU v7x, 32 devices: a whole 2x2x4 slice. The times are simulated.
32 devices in a mesh: groups: 2 (over y), seq: 4 (over x, core), sub: 4 (over z).
Axes of the slice: x: 2, y: 2, z: 4, core: 2. Of those that a mesh axis runs over, the one named last changes fastest.
Arguments:
- queries: bfloat16 [16384, 1024], P(('groups', 'seq', 'sub')), parts along dimension 0, may hold values from -6 to 6
- key_vectors: bfloat16 [16384, 1024], P(('groups', 'seq', 'sub')), parts along dimension 0, may hold values from -6 to 6
- value_vectors: bfloat16 [16384, 1024], P(('groups', 'seq', 'sub')), parts along dimension 0, may hold values from -16 to 16
- cotangent: bfloat16 [16384, 1024], P(('groups', 'seq', 'sub')), parts along dimension 0, may hold values from -6 to 6
- norm_gain: float32 [1024], replicated, may hold values from 0.1 to 1.9
Outputs:
- attended_out: bfloat16 [16384, 1024], P(('groups', 'seq', 'sub')), parts along dimension 0
- query_grad: bfloat16 [16384, 1024], P(('groups', 'seq', 'sub')), parts along dimension 0
- key_grad: bfloat16 [16384, 1024], P(('groups', 'seq', 'sub')), parts along dimension 0
- value_grad: bfloat16 [16384, 1024], P(('groups', 'seq', 'sub')), parts along dimension 0
There are 2 independent parts, one for each index of `groups`. A program takes and returns all parts, laid end to end along the dimension named above; an argument that names none is the same for every part. Nothing has to cross between parts.
All inputs are finite; a program needn't handle non-finite values.
Results may differ from a plain program's by a relative error of at most 0.0058.
Values sent between devices are 32-bit elements; how exact they have to be, the bound alone decides.
A program may use at most 192 MiB of HBM per device.

v0:
```python
from functools import partial

import jax
import jax.numpy as jnp
from jax import lax
from jax.sharding import PartitionSpec as P

H = 8
DH = 128
BLK = 512


def entering(part, axis, combine, identity, reverse):
    count = lax.axis_size(axis)
    place = lax.axis_index(axis)
    ahead = count - 1 - place if reverse else place
    gathered = lax.all_gather(part, axis)
    state = jnp.zeros_like(part) + jnp.asarray(identity, part.dtype)

    def one(turn, state):
        source = count - 1 - turn if reverse else turn
        return combine(state, lax.dynamic_index_in_dim(gathered, source, 0, False))

    return lax.fori_loop(0, ahead, one, state)


def normalize(attended, gain_heads):
    inverse = lax.rsqrt(jnp.mean(attended * attended, axis=-1, keepdims=True) + 1e-05)
    return attended * inverse * gain_heads


def add_states(first_part, second_part):
    return first_part + second_part


def forward_chain(overall):
    zeros_state = jnp.zeros_like(overall)
    return entering(overall, ("seq", "sub"), add_states, zeros_state, False)


def backward_chain(overall):
    zeros_state = jnp.zeros_like(overall)
    within = entering(overall, "sub", add_states, zeros_state, True)
    group_sum = lax.psum(overall, "sub")
    after_groups = entering(group_sum, "seq", add_states, zeros_state, True)
    return after_groups + within


def local(queries, key_vectors, value_vectors, cotangent, norm_gain):
    local_rows = queries.shape[0]
    num_blocks = local_rows // BLK
    shape_blocks = (num_blocks, BLK, H, DH)
    query_blocks = queries.reshape(shape_blocks)
    key_blocks = key_vectors.reshape(shape_blocks)
    value_blocks = value_vectors.reshape(shape_blocks)
    causal = (jnp.arange(BLK)[:, None] >= jnp.arange(BLK)[None, :])[None, None]
    gain_heads = norm_gain.reshape(H, DH)
    zero_block = jnp.zeros((1, H, DH, DH), jnp.float32)
    block_states = jnp.einsum(
        "bthd,bthe->bhde", key_blocks, value_blocks, preferred_element_type=jnp.float32
    )
    overall = jnp.sum(block_states, axis=0)
    earlier_sum = jnp.concatenate([zero_block, jnp.cumsum(block_states, axis=0)[:-1]], axis=0)
    scores = jnp.einsum(
        "bshd,bthd->bhst", query_blocks, key_blocks, preferred_element_type=jnp.float32
    )
    scores = jnp.where(causal, scores, 0.0).astype(jnp.bfloat16)
    intra = jnp.einsum("bhst,bthd->bshd", scores, value_blocks, preferred_element_type=jnp.float32)
    incoming = forward_chain(overall)
    states_low = (incoming[None] + earlier_sum).astype(jnp.bfloat16)
    attended = intra + jnp.einsum(
        "bshd,bhde->bshe", query_blocks, states_low, preferred_element_type=jnp.float32
    )
    normed, pullback = jax.vjp(partial(normalize, gain_heads=gain_heads), attended)
    attended_out = normed.astype(jnp.bfloat16).reshape(local_rows, H * DH)
    grad_blocks = pullback(cotangent.astype(jnp.float32).reshape(shape_blocks))[0].astype(
        jnp.bfloat16
    )
    block_grads = jnp.einsum(
        "bshd,bshe->bhde", query_blocks, grad_blocks, preferred_element_type=jnp.float32
    )
    overall_grad = jnp.sum(block_grads, axis=0)
    reversed_sum = jnp.cumsum(block_grads[::-1], axis=0)[::-1]
    later_sum = jnp.concatenate([reversed_sum[1:], zero_block], axis=0)
    grad_scores = jnp.einsum(
        "bshe,bthe->bhst", grad_blocks, value_blocks, preferred_element_type=jnp.float32
    )
    grad_scores = jnp.where(causal, grad_scores, 0.0).astype(jnp.bfloat16)
    query_grad = jnp.einsum(
        "bhst,bthd->bshd", grad_scores, key_blocks, preferred_element_type=jnp.float32
    )
    query_grad = query_grad + jnp.einsum(
        "bshe,bhde->bshd", grad_blocks, states_low, preferred_element_type=jnp.float32
    )
    key_intra = jnp.einsum(
        "bhst,bshd->bthd", grad_scores, query_blocks, preferred_element_type=jnp.float32
    )
    value_intra = jnp.einsum(
        "bhst,bshe->bthe", scores, grad_blocks, preferred_element_type=jnp.float32
    )
    incoming_grad = backward_chain(overall_grad)
    after_low = (incoming_grad[None] + later_sum).astype(jnp.bfloat16)
    key_grad = key_intra + jnp.einsum(
        "bthe,bhde->bthd", value_blocks, after_low, preferred_element_type=jnp.float32
    )
    value_grad = value_intra + jnp.einsum(
        "bthd,bhde->bthe", key_blocks, after_low, preferred_element_type=jnp.float32
    )
    return (
        attended_out,
        query_grad.astype(jnp.bfloat16).reshape(local_rows, H * DH),
        key_grad.astype(jnp.bfloat16).reshape(local_rows, H * DH),
        value_grad.astype(jnp.bfloat16).reshape(local_rows, H * DH),
    )


def solution(mesh):
    return jax.shard_map(
        local,
        mesh=mesh,
        in_specs=(
            P(("groups", "seq", "sub"), None),
            P(("groups", "seq", "sub"), None),
            P(("groups", "seq", "sub"), None),
            P(("groups", "seq", "sub"), None),
            P(),
        ),
        out_specs=(
            P(("groups", "seq", "sub"), None),
            P(("groups", "seq", "sub"), None),
            P(("groups", "seq", "sub"), None),
            P(("groups", "seq", "sub"), None),
        ),
        check_vma=False,
    )
```

profile of v0, /device:TPU:0, one launch (start us, length us, event | category | flops | bytes accessed | tf_op | source)
XLA Modules:
  0.0 246.2 jit_solution(12527830340978940693)
XLA Ops:
  7.2 1.6 copy.62
  10.5 1.2 fusion.12
  11.7 2.7 %copy.39 = f32[512,1024]{0,1:T(8,128)} copy(bf16[512,1024]{1,0:T(8,128)(2,1)} %param.14) | data formatting | bytes 3145728 | tf_op jit(solution)/shard_map/reshape | solution.py:76
  14.5 4.5 %select_convert_fusion.1 = bf16[8,512,512]{2,1,0:T(8,128)(2,1)} fusion(pred[512,512]{1,0:T(8,128)(4,1)S(1)} %iota_compare_fusion, bf16[512,1024]{1,0:T(8,128)(2,1)} %param.12, bf16[512,1024]{1,0:T(8,128)(2,1)S(1)} %copy-done.3), kind=kOutput, calls=%fused_computation.4 | convolution fusion | flops 541065216 | bytes 6553600 | tf_op jit(solution)/shard_map/bshd,bthd->bhst/dot_general | solution.py:64
  19.0 70.5 %all-gather.8.cloned.1.call-done = f32[128,128,128]{2,1,0:T(8,128)} async-done(((f32[8,128,128]{2,1,0:T(8,128)}), f32[128,128,128]{2,1,0:T(8,128)}) %all-gather.8.cloned.1.call-update) | async-done | bytes 8388624 | tf_op jit(solution)/shard_map/all_gather | solution.py:17
  91.1 3.8 %fusion.6 = (f32[512,8]{0,1:T(8,128)S(1)}, f32[512,8]{0,1:T(8,128)S(1)}, f32[8,128,512]{2,1,0:T(8,128)S(1)}) fusion(f32[1,512,8,128]{1,3,2,0:T(8,128)S(1)} %bitcast.139, f32[8,128]{1,0:T(8,128)S(1)} %bitcast.150, f32[8,128,512]{2,1,0:T(8,128)S(1)} %fusion.20, bf16[8,512,512]{2,1,0:T(8,128)(2,1)} %select_convert_fusion.1, bf16[512,1024]{1,0:T(8,128)(2,1)S(1)} %copy-done), kind=kOutput, calls=%fused_computation.18 | convolution fusion | flops 540008448 | bytes 11571200 | tf_op jit(solution)/shard_map/bhst,bthd->bshd/dot_general | solution.py:68
  95.0 1.7 fusion.7
  99.7 56.6 %all-reduce.2.cloned.1.call-done = f32[1,8,128,128]{2,3,1,0:T(8,128)} async-done(((f32[1,8,128,128]{2,3,1,0:T(8,128)}), f32[1,8,128,128]{2,3,1,0:T(8,128)}) %all-reduce.2.cloned.1.call-update) | async-done | bytes 524304 | tf_op jit(solution)/shard_map/psum | solution.py:44
  156.3 2.0 copy.46
  158.8 1.4 select_convert_fusion
  160.3 2.5 fusion.2
  162.7 2.3 copy.52
  165.0 2.3 copy.51
  167.3 4.3 %fusion.36 = f32[8,128,512]{2,1,0:T(8,128)} fusion(bf16[512,8,128]{0,2,1:T(8,128)(2,1)S(1)} %get-tuple-element.184, bf16[8,512,512]{2,1,0:T(8,128)(2,1)} %select_convert_fusion.1), kind=kOutput, calls=%fused_computation.54 | convolution fusion | flops 536870912 | bytes 7340032 | tf_op jit(solution)/shard_map/bhst,bshe->bthe/dot_general | solution.py:98
  171.6 32.3 %all-gather.10.cloned.1.call-done = f32[32,128,128]{2,1,0:T(8,128)} async-done(((f32[8,128,128]{2,1,0:T(8,128)}), f32[32,128,128]{2,1,0:T(8,128)}) %all-gather.10.cloned.1.call-update) | async-done | bytes 2097168 | tf_op jit(solution)/shard_map/all_gather | solution.py:17
  203.9 3.6 %while.36 = (s32[]{:T(128)}, f32[8,128,128]{2,1,0:T(8,128)S(1)}, s32[]{:T(128)}, f32[4,8,128,128]{3,2,1,0:T(8,128)}, s32[]{:T(128)}, /*index=5*/s32[]{:T(128)}, s32[]{:T(128)}, s32[]{:T(128)}) while((s32[]{:T(128)}, f32[8,128,128]{2,1,0:T(8,128)S(1)}, s32[]{:T(128)}, f32[4,8,128,128]{3,2,1,0:T(8,128)}, s32[]{:T(128)}, /*index=5*/s32[]{:T(128)}, ...), condition=%wide.region_8.9_spmd, body=%wide.region_7.8_spmd.sunk | while | flops 131078 | bytes 1572999 | solution.py:24
  203.9 1.2 bitcast_add_fusion.11
  207.5 19.1 %all-gather.6.cloned.1.call-done = f32[4,8,128,128]{3,2,1,0:T(8,128)} async-done(((f32[1,8,128,128]{3,2,1,0:T(8,128)}), f32[4,8,128,128]{3,2,1,0:T(8,128)}) %all-gather.6.cloned.1.call-update) | async-done | bytes 2097168 | tf_op jit(solution)/shard_map/all_gather | solution.py:17
  226.6 3.6 %while.35 = (s32[]{:T(128)}, f32[8,128,128]{2,1,0:T(8,128)S(1)}, s32[]{:T(128)}, f32[4,8,128,128]{3,2,1,0:T(8,128)}, s32[]{:T(128)}, /*index=5*/s32[]{:T(128)}, s32[]{:T(128)}, s32[]{:T(128)}) while((s32[]{:T(128)}, f32[8,128,128]{2,1,0:T(8,128)S(1)}, s32[]{:T(128)}, f32[4,8,128,128]{3,2,1,0:T(8,128)}, s32[]{:T(128)}, /*index=5*/s32[]{:T(128)}, ...), condition=%wide.region_6.7_spmd, body=%wide.region_5.6_spmd.sunk | while | flops 131078 | bytes 1572999 | solution.py:24
  226.7 1.2 bitcast_add_fusion.10
  230.3 1.8 fusion.9
  233.4 1.3 copy.54
  234.7 3.7 %fusion.1 = bf16[8,128,512]{2,1,0:T(8,128)(2,1)S(1)} fusion(f32[8,128,512]{2,1,0:T(8,128)} %fusion.9, bf16[8,512,512]{2,1,0:T(8,128)(2,1)} %copy-done.2, bf16[512,1024]{1,0:T(8,128)(2,1)S(1)} %copy-done.5), kind=kOutput, calls=%fused_computation.8 | convolution fusion | flops 537919488 | bytes 8388608 | tf_op jit(solution)/shard_map/bhst,bshd->bthd/dot_general | solution.py:95
  238.4 1.3 copy.53
  (49 shorter events, 12.9 us)
Async XLA Ops:
  7.2 3.3 %copy-start = (bf16[512,1024]{1,0:T(8,128)(2,1)S(1)}, bf16[512,1024]{1,0:T(8,128)(2,1)}, u32[]{:S(2)}) copy-start(bf16[512,1024]{1,0:T(8,128)(2,1)} %param.13) | copy-start | bytes 3145732
  7.2 82.3 %all-gather.8.cloned.1.call-start = ((), (), s32[]{:S(2)}) async-start(), calls=%async_computation.2 | async-start | bytes 8912896 | tf_op jit(solution)/shard_map/all_gather | solution.py:17
  9.5 1.0 copy-start.6
  11.7 2.8 %copy-start.3 = (bf16[512,1024]{1,0:T(8,128)(2,1)S(1)}, bf16[512,1024]{1,0:T(8,128)(2,1)}, u32[]{:S(2)}) copy-start(bf16[512,1024]{1,0:T(8,128)(2,1)} %param.11) | copy-start | bytes 3145732
  89.5 1.6 copy-start.1
  89.5 1.6 copy-start.11
  95.0 1.7 copy-start.4
  97.2 1.0 copy-start.9
  98.2 58.2 %all-reduce.2.cloned.1.call-start = ((), (), s32[]{:S(2)}) async-start(), calls=%async_computation | async-start | bytes 1048576 | tf_op jit(solution)/shard_map/psum | solution.py:44
  98.9 105.0 %all-gather.10.cloned.1.call-start = ((), (), s32[]{:S(2)}) async-start(), calls=%async_computation.3 | async-start | bytes 2621440 | tf_op jit(solution)/shard_map/all_gather | solution.py:17
  99.6 127.0 %all-gather.6.cloned.1.call-start = ((), (), s32[]{:S(2)}) async-start(), calls=%async_computation.1 | async-start | bytes 2621440 | tf_op jit(solution)/shard_map/all_gather | solution.py:17
  158.8 1.4 copy-start.7
  160.3 2.5 %copy-start.2 = (bf16[8,512,512]{2,1,0:T(8,128)(2,1)}, bf16[8,512,512]{2,1,0:T(8,128)(2,1)S(1)}, u32[]{:S(2)}) copy-start(bf16[8,512,512]{2,1,0:T(8,128)(2,1)S(1)} %select_convert_fusion) | copy-start | bytes 12582916
  230.2 1.9 copy-start.8
  230.3 2.6 %copy-start.10 = (bf16[512,1024]{1,0:T(8,128)(2,1)S(1)}, bf16[512,1024]{1,0:T(8,128)(2,1)}, u32[]{:S(2)}) copy-start(bf16[512,1024]{1,0:T(8,128)(2,1)} %param.12) | copy-start | bytes 3145732
  233.4 1.3 copy-start.5
Sparse Core Ops, SparseCore 0:
  11.9 77.5 all-gather.7
  101.9 54.3 all-reduce.1
  157.9 45.9 all-gather.9
  205.3 21.2 all-gather.5
where the time goes:
time: 247 us; the launch traced here: 246 us
  waiting for transfers between devices  180 us (73%)
  matrix products  25 us (10%)
  local copies, waits for them, and re-layouts  18.1 us (7%)
  between operations  14 us (6%)
  other arithmetic  8.86 us (4%)
    all_gather x3, waiting for transfers between devices, entering(): gathered = lax.all_gather(part, axis)  122 us
    psum x1, waiting for transfers between devices, backward_chain(): group_sum = lax.psum(overall, 'sub')  56.6 us
    unnamed x29, local copies, waits for them, and re-layouts  11.6 us
    add x6, other arithmetic, add_states(): return first_part + second_part  7.01 us
  transfers between devices with their start and end apart: 4, of which 4 were waited for; matrix products, arithmetic and copies ran while one was open for 11% of the time, Pallas kernels for 0%

commit v1 on v0

v1 whole, which is shorter than its diff:
```python
import functools

import jax
import jax.numpy as jnp
from jax import lax
from jax.experimental import pallas as pl
from jax.experimental.pallas import tpu as pltpu
from jax.sharding import PartitionSpec as P

H = 8
DH = 128
BLK = 512
MESH = pl.DeviceIdType.MESH


def mm(a, b, ca, cb):
    return lax.dot_general(a, b, (((ca,), (cb,)), ((), ())), preferred_element_type=jnp.float32)


def kernel(
    n_seq, n_sub, q_ref, k_ref, v_ref, c_ref, gain_ref,
    out_ref, dq_ref, dk_ref, dv_ref,
    part, pieces, sums, enter, back_part, back_pieces, back_sums, back_enter,
    scores, attended, grad, dk_part, dv_part,
    send_sems, recv_sems,
):
    count = n_seq * n_sub
    rows = H * DH // count
    me = lax.axis_index("seq") * n_sub + lax.axis_index("sub")

    def where(peer):
        return {"seq": peer // n_sub, "sub": lax.rem(peer, n_sub)}

    def other(step):
        return lax.rem(me + step, count)

    def head(h):
        return pl.ds(pl.multiple_of(h * DH, DH), DH)

    def chunk(owner):
        return pl.ds(pl.multiple_of(owner * rows, rows), rows)

    barrier = pltpu.get_barrier_semaphore()

    @pl.loop(1, count)
    def _(step):
        pl.semaphore_signal(barrier, inc=1, device_id=where(other(step)), device_id_type=MESH)

    def drain(buffer, sem):
        whole = buffer.at[pl.ds(0, count - 1)]
        pltpu.make_async_copy(whole, whole, sem).wait()

    def spread(source, landing, phase):
        @pl.loop(1, count)
        def _(step):
            peer = other(step)
            pltpu.make_async_remote_copy(
                src_ref=source.at[chunk(peer)],
                dst_ref=landing.at[me],
                send_sem=send_sems.at[phase],
                recv_sem=recv_sems.at[phase],
                device_id=where(peer),
                device_id_type=MESH,
            ).start()

    def give_back(landing, totals, result, phase, reverse):
        def add_up(turn, total):
            peer = count - 1 - turn if reverse else turn
            totals[peer] = total
            return total + landing[peer]

        lax.fori_loop(0, count, add_up, jnp.zeros((rows, DH), jnp.float32))

        @pl.loop(1, count)
        def _(step):
            peer = other(step)
            pltpu.make_async_remote_copy(
                src_ref=totals.at[peer],
                dst_ref=result.at[chunk(me)],
                send_sem=send_sems.at[phase],
                recv_sem=recv_sems.at[phase],
                device_id=where(peer),
                device_id_type=MESH,
            ).start()

        result[chunk(me), :] = totals[me]

    @pl.loop(0, H)
    def _(h):
        part[head(h), :] = mm(k_ref[:, head(h)], v_ref[:, head(h)], 0, 0)

    pieces[me] = part[chunk(me), :]
    pl.semaphore_wait(barrier, count - 1)
    spread(part, pieces, 0)

    causal = lax.broadcasted_iota(jnp.int32, (BLK, BLK), 0) >= lax.broadcasted_iota(
        jnp.int32, (BLK, BLK), 1
    )

    @pl.loop(0, H)
    def _(h):
        s = mm(q_ref[:, head(h)], k_ref[:, head(h)], 1, 1)
        scores[h] = jnp.where(causal, s, 0.0).astype(jnp.bfloat16)

    drain(pieces, recv_sems.at[0])
    give_back(pieces, sums, enter, 1, False)

    @pl.loop(0, H)
    def _(h):
        attended[:, head(h)] = mm(scores[h], v_ref[:, head(h)], 1, 0)

    drain(pieces, recv_sems.at[1])

    @pl.loop(0, H)
    def _(h):
        q = q_ref[:, head(h)]
        att = attended[:, head(h)] + mm(q, enter[head(h), :].astype(jnp.bfloat16), 1, 0)
        inverse = lax.rsqrt(jnp.mean(att * att, axis=-1, keepdims=True) + 1e-05)
        gain = gain_ref[:, head(h)]
        out_ref[:, head(h)] = (att * inverse * gain).astype(jnp.bfloat16)
        scaled = c_ref[:, head(h)].astype(jnp.float32) * gain
        along = jnp.mean(scaled * att, axis=-1, keepdims=True) * inverse * inverse
        g = (inverse * (scaled - att * along)).astype(jnp.bfloat16)
        grad[:, head(h)] = g
        back_part[head(h), :] = mm(q, g, 0, 0)

    back_pieces[me] = back_part[chunk(me), :]
    spread(back_part, back_pieces, 2)

    @pl.loop(0, H)
    def _(h):
        g = grad[:, head(h)]
        s = mm(g, v_ref[:, head(h)], 1, 1)
        s = jnp.where(causal, s, 0.0).astype(jnp.bfloat16)
        dq = mm(s, k_ref[:, head(h)], 1, 0)
        dq = dq + mm(g, enter[head(h), :].astype(jnp.bfloat16), 1, 1)
        dq_ref[:, head(h)] = dq.astype(jnp.bfloat16)
        dk_part[:, head(h)] = mm(s, q_ref[:, head(h)], 0, 0)

    drain(back_pieces, recv_sems.at[2])
    give_back(back_pieces, back_sums, back_enter, 3, True)

    @pl.loop(0, H)
    def _(h):
        dv_part[:, head(h)] = mm(scores[h], grad[:, head(h)], 0, 0)

    drain(back_pieces, recv_sems.at[3])

    @pl.loop(0, H)
    def _(h):
        after = back_enter[head(h), :].astype(jnp.bfloat16)
        dk = dk_part[:, head(h)] + mm(v_ref[:, head(h)], after, 1, 1)
        dk_ref[:, head(h)] = dk.astype(jnp.bfloat16)
        dv = dv_part[:, head(h)] + mm(k_ref[:, head(h)], after, 1, 0)
        dv_ref[:, head(h)] = dv.astype(jnp.bfloat16)

    for phase in range(4):
        drain(pieces, send_sems.at[phase])


def local(n_seq, n_sub, queries, key_vectors, value_vectors, cotangent, norm_gain):
    count = n_seq * n_sub
    rows = H * DH // count
    width = H * DH
    vmem = pl.BlockSpec(memory_space=pltpu.VMEM)
    state = pltpu.VMEM((width, DH), jnp.float32)
    split = pltpu.VMEM((count, rows, DH), jnp.float32)
    wide = pltpu.VMEM((BLK, width), jnp.float32)
    return pl.pallas_call(
        functools.partial(kernel, n_seq, n_sub),
        out_shape=[jax.ShapeDtypeStruct((BLK, width), jnp.bfloat16)] * 4,
        in_specs=[vmem] * 5,
        out_specs=[vmem] * 4,
        scratch_shapes=[
            state, split, split, state, state, split, split, state,
            pltpu.VMEM((H, BLK, BLK), jnp.bfloat16),
            wide,
            pltpu.VMEM((BLK, width), jnp.bfloat16),
            wide,
            wide,
            pltpu.SemaphoreType.DMA((4,)),
            pltpu.SemaphoreType.DMA((4,)),
        ],
        compiler_params=pltpu.CompilerParams(
            collective_id=0, has_side_effects=True, vmem_limit_bytes=48 << 20
        ),
    )(queries, key_vectors, value_vectors, cotangent, norm_gain.reshape(1, width))


def solution(mesh):
    rows = P(("groups", "seq", "sub"), None)
    return jax.shard_map(
        functools.partial(local, mesh.shape["seq"], mesh.shape["sub"]),
        mesh=mesh,
        in_specs=(rows, rows, rows, rows, P()),
        out_specs=(rows, rows, rows, rows),
        check_vma=False,
    )
```

time: 247 us -> 71.3 us (0.29)
  waiting for transfers between devices: 180 us -> 0 us
  Pallas kernels: 0 us -> 64.6 us
  matrix products: 25 us -> 0 us
  between operations: 14 us -> 0.65 us
  local copies, waits for them, and re-layouts: 18.1 us -> 5.79 us
  other arithmetic: 8.86 us -> 0 us
    all_gather x3 -> x0, waiting for transfers between devices: 122 us -> none  [entering(): gathered = lax.all_gather(part, axis)]
    pallas_call x0 -> x1, Pallas kernels: none -> 64.6 us  [local(): pl.pallas_call(functools.partial(kernel, n_seq, n_sub), out_shape=[jax.Sh...]
    psum x1 -> x0, waiting for transfers between devices: 56.6 us -> none  [backward_chain(): group_sum = lax.psum(overall, 'sub')]
    dot_general x12 -> x0, matrix products: 25 us -> none  [the longest x1 4.5 us: local(): jnp.einsum('bshd,bthd->bhst', query_blocks, key_blocks, preferred_element...]
    add x6 -> x0, other arithmetic: 7.01 us -> none  [add_states(): return first_part + second_part]
    unnamed x29 -> x8, local copies, waits for them, and re-layouts: 11.6 us -> 5.79 us
    reshape x1 -> x0, local copies, waits for them, and re-layouts: 2.68 us -> none  [local(): cotangent.astype(jnp.float32).reshape(shape_blocks)]
  transfers between devices with their start and end apart: 4 -> 0, of which waited for: 4 -> 0; matrix products, arithmetic and copies ran while one was open for 11% -> 0% of each run, Pallas kernels for 0% -> 0%
where the time goes in v1:
time: 71.3 us; the launch traced here: 71.1 us
  Pallas kernels  64.6 us (91%)
  local copies, waits for them, and re-layouts  5.79 us (8%)
    pallas_call x1, Pallas kernels, local(): pl.pallas_call(functools.partial(kernel, n_seq, n_sub), out_shape=[jax.Sh...  64.6 us
    unnamed x8, local copies, waits for them, and re-layouts  5.79 us

profile of v1, /device:TPU:0, one launch (start us, length us, event | category | flops | bytes accessed | tf_op | source)
XLA Modules:
  0.0 71.1 jit_solution(9271174886565963824)
XLA Ops:
  0.6 0.0 copy-start
  0.6 1.2 %copy-done = bf16[512,1024]{1,0:T(8,128)(2,1)S(1)} copy-done((bf16[512,1024]{1,0:T(8,128)(2,1)S(1)}, bf16[512,1024]{1,0:T(8,128)(2,1)}, u32[]{:S(2)}) %copy-start) | copy-done | bytes 1048600
  1.9 0.0 copy-start.1
  1.9 0.7 copy-done.1
  2.5 64.6 %shard_map.84 = (bf16[512,1024]{1,0:T(8,128)(2,1)S(1)}, bf16[512,1024]{1,0:T(8,128)(2,1)S(1)}, bf16[512,1024]{1,0:T(8,128)(2,1)S(1)}, bf16[512,1024]{1,0:T(8,128)(2,1)S(1)}) custom-call(bf16[512,1024]{1,0:T(8,128)(2,1)S(1)} %copy-done, bf16[512,1024]{1,0:T(8,128)(2,1)} %k_ref.1, bf16[512,1024]{1,0:T(8,128)(2,1)} %v_ref.1, bf16[512,1024]{1,0:T(8,128)(2,1)} %c_ref.1, ...), custom_call_target="tpu_custom_call" | custom-call | tf_op jit(solution)/shard_map/pallas_call | solution.py:169
  67.2 1.0 %copy.13 = bf16[512,1024]{1,0:T(8,128)(2,1)} copy(bf16[512,1024]{1,0:T(8,128)(2,1)S(1)} %get-tuple-element.8) | data formatting | bytes 2097152
  68.2 1.0 %copy.14 = bf16[512,1024]{1,0:T(8,128)(2,1)} copy(bf16[512,1024]{1,0:T(8,128)(2,1)S(1)} %get-tuple-element.9) | data formatting | bytes 2097152
  69.1 1.0 %copy.15 = bf16[512,1024]{1,0:T(8,128)(2,1)} copy(bf16[512,1024]{1,0:T(8,128)(2,1)S(1)} %get-tuple-element.10) | data formatting | bytes 2097152
  70.1 1.0 %copy.16 = bf16[512,1024]{1,0:T(8,128)(2,1)} copy(bf16[512,1024]{1,0:T(8,128)(2,1)S(1)} %get-tuple-element.11) | data formatting | bytes 2097152
Async XLA Ops:
  0.6 1.2 %copy-start = (bf16[512,1024]{1,0:T(8,128)(2,1)S(1)}, bf16[512,1024]{1,0:T(8,128)(2,1)}, u32[]{:S(2)}) copy-start(bf16[512,1024]{1,0:T(8,128)(2,1)} %q_ref.1) | copy-start | bytes 3145732
  1.9 0.7 copy-start.1

commit v2 on v1

v2 whole, which is shorter than its diff:
```python
import functools

import jax
import jax.numpy as jnp
from jax import lax
from jax.experimental import pallas as pl
from jax.experimental.pallas import tpu as pltpu
from jax.sharding import PartitionSpec as P

H = 8
DH = 128
BLK = 512
SUB_SKEW = 2
SEQ_SKEW = 1
MESH = pl.DeviceIdType.MESH


def mm(a, b, ca, cb):
    return lax.dot_general(a, b, (((ca,), (cb,)), ((), ())), preferred_element_type=jnp.float32)


def kernel(
    n_seq, n_sub, q_ref, k_ref, v_ref, c_ref, gain_ref,
    out_ref, dq_ref, dk_ref, dv_ref,
    own, up_in, up_out, down_in, down_out, seq_in, seq_out,
    scores, attended, grad, dk_part, dv_part,
    send_sems, recv_sems,
):
    row = lax.axis_index("seq")
    place = lax.axis_index("sub")
    has_prev, has_next = place > 0, place < n_sub - 1
    has_prev_row, has_next_row = row > 0, row < n_seq - 1
    depth = SUB_SKEW * (n_sub - 1) + SEQ_SKEW * (n_seq - 1)

    def head(h):
        return pl.ds(pl.multiple_of(h * DH, DH), DH)

    def at_sub(step):
        return {"sub": place + step}

    def at_seq(step):
        return {"seq": row + step}

    barrier = pltpu.get_barrier_semaphore()
    neighbours = (
        (has_prev, at_sub(-1)), (has_next, at_sub(1)),
        (has_prev_row, at_seq(-1)), (has_next_row, at_seq(1)),
    )
    for exists, device in neighbours:
        @pl.when(exists)
        def _(device=device):
            pl.semaphore_signal(barrier, inc=1, device_id=device, device_id_type=MESH)

    first_row = (jnp.logical_not(has_prev_row), jnp.logical_not(has_next_row))
    for scan in range(2):
        for empty, buffer in (
            (jnp.logical_not(has_prev), up_in),
            (jnp.logical_not(has_next), down_in),
            (first_row[scan], seq_in),
        ):
            @pl.when(empty)
            def _(buffer=buffer, scan=scan):
                buffer[scan] = jnp.zeros((H, DH, DH), jnp.float32)

    def hop(source, landing, scan, kind, h, device):
        return pltpu.make_async_remote_copy(
            src_ref=source.at[scan, h],
            dst_ref=landing.at[scan, h],
            send_sem=send_sems.at[scan, kind],
            recv_sem=recv_sems.at[scan, kind, h],
            device_id=device,
            device_id_type=MESH,
        )

    def in_turn(h, body):
        @pl.when(jnp.logical_and(h >= 0, h < H))
        def _():
            body(h)

    def link(landing, source, scan, kind, h, arrives, leaves, step, value):
        @pl.when(arrives)
        def _():
            hop(source, landing, scan, kind, h, step).wait_recv()

        source[scan, h] = value()

        @pl.when(leaves)
        def _():
            hop(source, landing, scan, kind, h, step).start()

    def up(scan):
        def body(h):
            link(up_in, up_out, scan, 0, h, has_prev, has_next, at_sub(1),
                 lambda: up_in[scan, h] + own[scan, h])
        return body

    def down(scan):
        def body(h):
            link(down_in, down_out, scan, 1, h, has_next, has_prev, at_sub(-1),
                 lambda: down_in[scan, h] + own[scan, h])
        return body

    def along_seq(scan):
        arrives, leaves, step = (
            (has_prev_row, has_next_row, at_seq(1)),
            (has_next_row, has_prev_row, at_seq(-1)),
        )[scan]

        def body(h):
            link(seq_in, seq_out, scan, 2, h, arrives, leaves, step,
                 lambda: seq_in[scan, h] + (up_out[scan, h] + down_in[scan, h]))
        return body

    def entering(scan, h):
        within = (up_in, down_in)[scan]
        return (seq_in[scan, h] + within[scan, h]).astype(jnp.bfloat16)

    def key_value_state(h):
        own[0, h] = mm(k_ref[:, head(h)], v_ref[:, head(h)], 0, 0)

    causal = lax.broadcasted_iota(jnp.int32, (BLK, BLK), 0) >= lax.broadcasted_iota(
        jnp.int32, (BLK, BLK), 1
    )

    def within_block(h):
        s = mm(q_ref[:, head(h)], k_ref[:, head(h)], 1, 1)
        s = jnp.where(causal, s, 0.0).astype(jnp.bfloat16)
        scores[h] = s
        attended[:, head(h)] = mm(s, v_ref[:, head(h)], 1, 0)

    def norm_and_pullback(h):
        q = q_ref[:, head(h)]
        att = attended[:, head(h)] + mm(q, entering(0, h), 1, 0)
        inverse = lax.rsqrt(jnp.mean(att * att, axis=-1, keepdims=True) + 1e-05)
        gain = gain_ref[:, head(h)]
        out_ref[:, head(h)] = (att * inverse * gain).astype(jnp.bfloat16)
        scaled = c_ref[:, head(h)].astype(jnp.float32) * gain
        along = jnp.mean(scaled * att, axis=-1, keepdims=True) * inverse * inverse
        g = (inverse * (scaled - att * along)).astype(jnp.bfloat16)
        grad[:, head(h)] = g
        own[1, h] = mm(q, g, 0, 0)

    def gradients_within(h):
        g = grad[:, head(h)]
        s = mm(g, v_ref[:, head(h)], 1, 1)
        s = jnp.where(causal, s, 0.0).astype(jnp.bfloat16)
        dq = mm(s, k_ref[:, head(h)], 1, 0) + mm(g, entering(0, h), 1, 1)
        dq_ref[:, head(h)] = dq.astype(jnp.bfloat16)
        dk_part[:, head(h)] = mm(s, q_ref[:, head(h)], 0, 0)
        dv_part[:, head(h)] = mm(scores[h], g, 0, 0)

    def finish(h):
        after = entering(1, h)
        dk = dk_part[:, head(h)] + mm(v_ref[:, head(h)], after, 1, 1)
        dk_ref[:, head(h)] = dk.astype(jnp.bfloat16)
        dv = dv_part[:, head(h)] + mm(k_ref[:, head(h)], after, 1, 0)
        dv_ref[:, head(h)] = dv.astype(jnp.bfloat16)

    key_value_state(0)
    behind = n_sub - 1 - place
    greeted = jnp.minimum(place, 1) + jnp.minimum(behind, 1)
    greeted = greeted + jnp.minimum(row, 1) + jnp.minimum(n_seq - 1 - row, 1)
    pl.semaphore_wait(barrier, greeted)
    turns = (row, n_seq - 1 - row)

    @pl.loop(0, H + 2 * depth + 1)
    def _(slot):
        for scan, start in ((0, 0), (1, depth + 1)):
            now = slot - start
            in_turn(now - SUB_SKEW * place, up(scan))
            in_turn(now - SUB_SKEW * behind, down(scan))
            in_turn(now - SUB_SKEW * jnp.maximum(place, behind) - SEQ_SKEW * turns[scan], along_seq(scan))
        in_turn(slot + 1, key_value_state)
        in_turn(slot - depth, norm_and_pullback)
        in_turn(slot - 1, within_block)
        in_turn(slot - depth - 2, gradients_within)
        in_turn(slot - 2 * depth - 1, finish)

    for scan in range(2):
        leaves_seq = (has_next_row, has_prev_row)[scan]
        for kind, leaves, source in (
            (0, has_next, up_out), (1, has_prev, down_out), (2, leaves_seq, seq_out),
        ):
            @pl.when(leaves)
            def _(kind=kind, source=source, scan=scan):
                whole = source.at[scan]
                pltpu.make_async_copy(whole, whole, send_sems.at[scan, kind]).wait()


def local(n_seq, n_sub, queries, key_vectors, value_vectors, cotangent, norm_gain):
    width = H * DH
    vmem = pl.BlockSpec(memory_space=pltpu.VMEM)
    states = pltpu.VMEM((2, H, DH, DH), jnp.float32)
    wide = pltpu.VMEM((BLK, width), jnp.float32)
    return pl.pallas_call(
        functools.partial(kernel, n_seq, n_sub),
        out_shape=[jax.ShapeDtypeStruct((BLK, width), jnp.bfloat16)] * 4,
        in_specs=[vmem] * 5,
        out_specs=[vmem] * 4,
        scratch_shapes=[
            *[states] * 7,
            pltpu.VMEM((H, BLK, BLK), jnp.bfloat16),
            wide,
            pltpu.VMEM((BLK, width), jnp.bfloat16),
            wide,
            wide,
            pltpu.SemaphoreType.DMA((2, 3)),
            pltpu.SemaphoreType.DMA((2, 3, H)),
        ],
        compiler_params=pltpu.CompilerParams(
            collective_id=0, has_side_effects=True, vmem_limit_bytes=48 << 20
        ),
    )(queries, key_vectors, value_vectors, cotangent, norm_gain.reshape(1, width))


def solution(mesh):
    rows = P(("groups", "seq", "sub"), None)
    return jax.shard_map(
        functools.partial(local, mesh.shape["seq"], mesh.shape["sub"]),
        mesh=mesh,
        in_specs=(rows, rows, rows, rows, P()),
        out_specs=(rows, rows, rows, rows),
        check_vma=False,
    )
```

time: 71.3 us -> 58 us (0.81)
  Pallas kernels: 64.6 us -> 51.4 us
    pallas_call x1, Pallas kernels: 64.6 us -> 51.4 us  [local(): pl.pallas_call(functools.partial(kernel, n_seq, n_sub), out_shape=[jax.Sh...]
where the time goes in v2:
time: 58 us; the launch traced here: 57.8 us
  Pallas kernels  51.4 us (89%)
  local copies, waits for them, and re-layouts  5.79 us (10%)
  between operations  0.65 us (1%)
    pallas_call x1, Pallas kernels, local(): pl.pallas_call(functools.partial(kernel, n_seq, n_sub), out_shape=[jax.Sh...  51.4 us
    unnamed x8, local copies, waits for them, and re-layouts  5.79 us

profile of v2, /device:TPU:0, one launch (start us, length us, event | category | flops | bytes accessed | tf_op | source)
XLA Modules:
  0.0 57.8 jit_solution(11825572333728286770)
XLA Ops:
  0.6 0.0 copy-start
  0.6 1.2 %copy-done = bf16[512,1024]{1,0:T(8,128)(2,1)S(1)} copy-done((bf16[512,1024]{1,0:T(8,128)(2,1)S(1)}, bf16[512,1024]{1,0:T(8,128)(2,1)}, u32[]{:S(2)}) %copy-start) | copy-done | bytes 1048600
  1.9 0.0 copy-start.1
  1.9 0.7 %copy-done.1 = f32[1024]{0:T(1024)S(1)} copy-done((f32[1024]{0:T(1024)S(1)}, f32[1024]{0:T(1024)}, u32[]{:S(2)}) %copy-start.1) | copy-done | bytes 4120
  2.5 51.4 %shard_map.84 = (bf16[512,1024]{1,0:T(8,128)(2,1)S(1)}, bf16[512,1024]{1,0:T(8,128)(2,1)S(1)}, bf16[512,1024]{1,0:T(8,128)(2,1)S(1)}, bf16[512,1024]{1,0:T(8,128)(2,1)S(1)}) custom-call(bf16[512,1024]{1,0:T(8,128)(2,1)S(1)} %copy-done, bf16[512,1024]{1,0:T(8,128)(2,1)} %k_ref.1, bf16[512,1024]{1,0:T(8,128)(2,1)} %v_ref.1, bf16[512,1024]{1,0:T(8,128)(2,1)} %c_ref.1, ...), custom_call_target="tpu_custom_call" | custom-call | tf_op jit(solution)/shard_map/pallas_call | solution.py:195
  53.9 1.0 %copy.13 = bf16[512,1024]{1,0:T(8,128)(2,1)} copy(bf16[512,1024]{1,0:T(8,128)(2,1)S(1)} %get-tuple-element.8) | data formatting | bytes 2097152
  54.9 1.0 %copy.14 = bf16[512,1024]{1,0:T(8,128)(2,1)} copy(bf16[512,1024]{1,0:T(8,128)(2,1)S(1)} %get-tuple-element.9) | data formatting | bytes 2097152
  55.9 1.0 %copy.15 = bf16[512,1024]{1,0:T(8,128)(2,1)} copy(bf16[512,1024]{1,0:T(8,128)(2,1)S(1)} %get-tuple-element.10) | data formatting | bytes 2097152
  56.8 1.0 %copy.16 = bf16[512,1024]{1,0:T(8,128)(2,1)} copy(bf16[512,1024]{1,0:T(8,128)(2,1)S(1)} %get-tuple-element.11) | data formatting | bytes 2097152
Async XLA Ops:
  0.6 1.2 %copy-start = (bf16[512,1024]{1,0:T(8,128)(2,1)S(1)}, bf16[512,1024]{1,0:T(8,128)(2,1)}, u32[]{:S(2)}) copy-start(bf16[512,1024]{1,0:T(8,128)(2,1)} %q_ref.1) | copy-start | bytes 3145732
  1.9 0.7 %copy-start.1 = (f32[1024]{0:T(1024)S(1)}, f32[1024]{0:T(1024)}, u32[]{:S(2)}) copy-start(f32[1024]{0:T(1024)} %param.9) | copy-start | bytes 12292

commit v3 on v2

--- a/solution.py
+++ b/solution.py
@@ -10,8 +10,9 @@
 H = 8
 DH = 128
 BLK = 512
-SUB_SKEW = 2
-SEQ_SKEW = 1
+PIECES = 2
+SUB_SKEW = 4
+SEQ_SKEW = 2
 MESH = pl.DeviceIdType.MESH
 
 
@@ -20,11 +21,12 @@
 
 
 def kernel(
-    n_seq, n_sub, q_ref, k_ref, v_ref, c_ref, gain_ref,
+    n_seq, n_sub, q_hbm, k_hbm, v_hbm, c_hbm, gain_hbm,
     out_ref, dq_ref, dk_ref, dv_ref,
+    q_ref, k_ref, v_ref, c_ref, gain_ref,
     own, up_in, up_out, down_in, down_out, seq_in, seq_out,
     scores, attended, grad, dk_part, dv_part,
-    send_sems, recv_sems,
+    send_sems, recv_sems, load_sems,
 ):
     row = lax.axis_index("seq")
     place = lax.axis_index("sub")
@@ -35,12 +37,25 @@
     def head(h):
         return pl.ds(pl.multiple_of(h * DH, DH), DH)
 
+    chunks, rows = H * PIECES, DH // PIECES
+
+    def piece(c):
+        return pl.ds(pl.multiple_of(c * rows, rows), rows)
+
     def at_sub(step):
         return {"sub": place + step}
 
     def at_seq(step):
         return {"seq": row + step}
 
+    loads = [
+        pltpu.make_async_copy(source, target, load_sems.at[index])
+        for index, (source, target) in enumerate(
+            ((k_hbm, k_ref), (v_hbm, v_ref), (q_hbm, q_ref), (c_hbm, c_ref), (gain_hbm, gain_ref))
+        )
+    ]
+    for load in loads:
+        load.start()
     barrier = pltpu.get_barrier_semaphore()
     neighbours = (
         (has_prev, at_sub(-1)), (has_next, at_sub(1)),
@@ -60,44 +75,51 @@
         ):
             @pl.when(empty)
             def _(buffer=buffer, scan=scan):
-                buffer[scan] = jnp.zeros((H, DH, DH), jnp.float32)
-
-    def hop(source, landing, scan, kind, h, device):
+                buffer[scan] = jnp.zeros((H * DH, DH), jnp.float32)
+
+    def hop(source, landing, scan, kind, c, device):
         return pltpu.make_async_remote_copy(
-            src_ref=source.at[scan, h],
-            dst_ref=landing.at[scan, h],
+            src_ref=source.at[scan, piece(c)],
+            dst_ref=landing.at[scan, piece(c)],
             send_sem=send_sems.at[scan, kind],
-            recv_sem=recv_sems.at[scan, kind, h],
+            recv_sem=recv_sems.at[scan, kind, c],
             device_id=device,
             device_id_type=MESH,
         )
 
-    def in_turn(h, body):
-        @pl.when(jnp.logical_and(h >= 0, h < H))
-        def _():
-            body(h)
-
-    def link(landing, source, scan, kind, h, arrives, leaves, step, value):
+    def in_turn(c, body):
+        @pl.when(jnp.logical_and(c >= 0, c < chunks))
+        def _():
+            body(c)
+
+    def head_turn(c, body):
+        due = jnp.logical_and(c >= 0, c < chunks)
+
+        @pl.when(jnp.logical_and(due, lax.rem(c, PIECES) == 0))
+        def _():
+            body(c // PIECES)
+
+    def link(landing, source, scan, kind, c, arrives, leaves, step, value):
         @pl.when(arrives)
         def _():
-            hop(source, landing, scan, kind, h, step).wait_recv()
-
-        source[scan, h] = value()
+            hop(source, landing, scan, kind, c, step).wait_recv()
+
+        source[scan, piece(c), :] = value()
 
         @pl.when(leaves)
         def _():
-            hop(source, landing, scan, kind, h, step).start()
+            hop(source, landing, scan, kind, c, step).start()
 
     def up(scan):
-        def body(h):
-            link(up_in, up_out, scan, 0, h, has_prev, has_next, at_sub(1),
-                 lambda: up_in[scan, h] + own[scan, h])
+        def body(c):
+            link(up_in, up_out, scan, 0, c, has_prev, has_next, at_sub(1),
+                 lambda: up_in[scan, piece(c), :] + own[scan, piece(c), :])
         return body
 
     def down(scan):
-        def body(h):
-            link(down_in, down_out, scan, 1, h, has_next, has_prev, at_sub(-1),
-                 lambda: down_in[scan, h] + own[scan, h])
+        def body(c):
+            link(down_in, down_out, scan, 1, c, has_next, has_prev, at_sub(-1),
+                 lambda: down_in[scan, piece(c), :] + own[scan, piece(c), :])
         return body
 
     def along_seq(scan):
@@ -106,17 +128,17 @@
             (has_next_row, has_prev_row, at_seq(-1)),
         )[scan]
 
-        def body(h):
-            link(seq_in, seq_out, scan, 2, h, arrives, leaves, step,
-                 lambda: seq_in[scan, h] + (up_out[scan, h] + down_in[scan, h]))
+        def body(c):
+            link(seq_in, seq_out, scan, 2, c, arrives, leaves, step,
+                 lambda: seq_in[scan, piece(c), :] + (up_out[scan, piece(c), :] + down_in[scan, piece(c), :]))
         return body
 
     def entering(scan, h):
         within = (up_in, down_in)[scan]
-        return (seq_in[scan, h] + within[scan, h]).astype(jnp.bfloat16)
+        return (seq_in[scan, head(h), :] + within[scan, head(h), :]).astype(jnp.bfloat16)
 
     def key_value_state(h):
-        own[0, h] = mm(k_ref[:, head(h)], v_ref[:, head(h)], 0, 0)
+        own[0, head(h), :] = mm(k_ref[:, head(h)], v_ref[:, head(h)], 0, 0)
 
     causal = lax.broadcasted_iota(jnp.int32, (BLK, BLK), 0) >= lax.broadcasted_iota(
         jnp.int32, (BLK, BLK), 1
@@ -138,7 +160,7 @@
         along = jnp.mean(scaled * att, axis=-1, keepdims=True) * inverse * inverse
         g = (inverse * (scaled - att * along)).astype(jnp.bfloat16)
         grad[:, head(h)] = g
-        own[1, h] = mm(q, g, 0, 0)
+        own[1, head(h), :] = mm(q, g, 0, 0)
 
     def gradients_within(h):
         g = grad[:, head(h)]
@@ -156,25 +178,29 @@
         dv = dv_part[:, head(h)] + mm(k_ref[:, head(h)], after, 1, 0)
         dv_ref[:, head(h)] = dv.astype(jnp.bfloat16)
 
+    loads[0].wait()
+    loads[1].wait()
     key_value_state(0)
+    for load in loads[2:]:
+        load.wait()
     behind = n_sub - 1 - place
     greeted = jnp.minimum(place, 1) + jnp.minimum(behind, 1)
     greeted = greeted + jnp.minimum(row, 1) + jnp.minimum(n_seq - 1 - row, 1)
     pl.semaphore_wait(barrier, greeted)
     turns = (row, n_seq - 1 - row)
 
-    @pl.loop(0, H + 2 * depth + 1)
+    @pl.loop(0, chunks + 2 * depth + PIECES)
     def _(slot):
-        for scan, start in ((0, 0), (1, depth + 1)):
+        for scan, start in ((0, 0), (1, depth + PIECES)):
             now = slot - start
             in_turn(now - SUB_SKEW * place, up(scan))
             in_turn(now - SUB_SKEW * behind, down(scan))
             in_turn(now - SUB_SKEW * jnp.maximum(place, behind) - SEQ_SKEW * turns[scan], along_seq(scan))
-        in_turn(slot + 1, key_value_state)
-        in_turn(slot - depth, norm_and_pullback)
-        in_turn(slot - 1, within_block)
-        in_turn(slot - depth - 2, gradients_within)
-        in_turn(slot - 2 * depth - 1, finish)
+        head_turn(slot + 1, key_value_state)
+        head_turn(slot - depth - PIECES + 1, norm_and_pullback)
+        head_turn(slot - 1, within_block)
+        head_turn(slot - depth - PIECES - 2, gradients_within)
+        head_turn(slot - 2 * depth - 2 * PIECES + 1, finish)
 
     for scan in range(2):
         leaves_seq = (has_next_row, has_prev_row)[scan]
@@ -190,14 +216,16 @@
 def local(n_seq, n_sub, queries, key_vectors, value_vectors, cotangent, norm_gain):
     width = H * DH
     vmem = pl.BlockSpec(memory_space=pltpu.VMEM)
-    states = pltpu.VMEM((2, H, DH, DH), jnp.float32)
+    states = pltpu.VMEM((2, width, DH), jnp.float32)
     wide = pltpu.VMEM((BLK, width), jnp.float32)
     return pl.pallas_call(
         functools.partial(kernel, n_seq, n_sub),
         out_shape=[jax.ShapeDtypeStruct((BLK, width), jnp.bfloat16)] * 4,
-        in_specs=[vmem] * 5,
+        in_specs=[pl.BlockSpec(memory_space=pl.ANY)] * 5,
         out_specs=[vmem] * 4,
         scratch_shapes=[
+            *[pltpu.VMEM((BLK, width), jnp.bfloat16)] * 4,
+            pltpu.VMEM((1, width), jnp.float32),
             *[states] * 7,
             pltpu.VMEM((H, BLK, BLK), jnp.bfloat16),
             wide,
@@ -205,7 +233,8 @@
             wide,
             wide,
             pltpu.SemaphoreType.DMA((2, 3)),
-            pltpu.SemaphoreType.DMA((2, 3, H)),
+            pltpu.SemaphoreType.DMA((2, 3, H * PIECES)),
+            pltpu.SemaphoreType.DMA((5,)),
         ],
         compiler_params=pltpu.CompilerParams(
             collective_id=0, has_side_effects=True, vmem_limit_bytes=48 << 20

time: 58 us -> 53.6 us (0.924)
  Pallas kernels: 51.4 us -> 47 us
    pallas_call x1, Pallas kernels: 51.4 us -> 47 us  [local(): pl.pallas_call(functools.partial(kernel, n_seq, n_sub), out_shape=[jax.Sh...]
where the time goes in v3:
time: 53.6 us; the launch traced here: 53.4 us
  Pallas kernels  47 us (88%)
  local copies, waits for them, and re-layouts  5.79 us (11%)
  between operations  0.65 us (1%)
    pallas_call x1, Pallas kernels, local(): pl.pallas_call(functools.partial(kernel, n_seq, n_sub), out_shape=[jax.Sh...  47 us
    unnamed x8, local copies, waits for them, and re-layouts  5.79 us

profile of v3, /device:TPU:0, one launch (start us, length us, event | category | flops | bytes accessed | tf_op | source)
XLA Modules:
  0.0 53.4 jit_solution(11196892543466031565)
XLA Ops:
  0.6 0.0 copy-start
  0.6 1.2 %copy-done = bf16[512,1024]{1,0:T(8,128)(2,1)S(1)} copy-done((bf16[512,1024]{1,0:T(8,128)(2,1)S(1)}, bf16[512,1024]{1,0:T(8,128)(2,1)}, u32[]{:S(2)}) %copy-start) | copy-done | bytes 1048600
  1.9 0.0 copy-start.1
  1.9 0.7 %copy-done.1 = f32[1024]{0:T(1024)S(1)} copy-done((f32[1024]{0:T(1024)S(1)}, f32[1024]{0:T(1024)}, u32[]{:S(2)}) %copy-start.1) | copy-done | bytes 4120
  2.5 47.0 %shard_map.84 = (bf16[512,1024]{1,0:T(8,128)(2,1)S(1)}, bf16[512,1024]{1,0:T(8,128)(2,1)S(1)}, bf16[512,1024]{1,0:T(8,128)(2,1)S(1)}, bf16[512,1024]{1,0:T(8,128)(2,1)S(1)}) custom-call(bf16[512,1024]{1,0:T(8,128)(2,1)S(1)} %copy-done, bf16[512,1024]{1,0:T(8,128)(2,1)} %k_hbm.1, bf16[512,1024]{1,0:T(8,128)(2,1)} %v_hbm.1, bf16[512,1024]{1,0:T(8,128)(2,1)} %c_hbm.1, ...), custom_call_target="tpu_custom_call" | custom-call | tf_op jit(solution)/shard_map/pallas_call | solution.py:221
  49.5 1.0 %copy.13 = bf16[512,1024]{1,0:T(8,128)(2,1)} copy(bf16[512,1024]{1,0:T(8,128)(2,1)S(1)} %get-tuple-element.8) | data formatting | bytes 2097152
  50.5 1.0 %copy.14 = bf16[512,1024]{1,0:T(8,128)(2,1)} copy(bf16[512,1024]{1,0:T(8,128)(2,1)S(1)} %get-tuple-element.9) | data formatting | bytes 2097152
  51.4 1.0 %copy.15 = bf16[512,1024]{1,0:T(8,128)(2,1)} copy(bf16[512,1024]{1,0:T(8,128)(2,1)S(1)} %get-tuple-element.10) | data formatting | bytes 2097152
  52.4 1.0 %copy.16 = bf16[512,1024]{1,0:T(8,128)(2,1)} copy(bf16[512,1024]{1,0:T(8,128)(2,1)S(1)} %get-tuple-element.11) | data formatting | bytes 2097152
Async XLA Ops:
  0.6 1.2 %copy-start = (bf16[512,1024]{1,0:T(8,128)(2,1)S(1)}, bf16[512,1024]{1,0:T(8,128)(2,1)}, u32[]{:S(2)}) copy-start(bf16[512,1024]{1,0:T(8,128)(2,1)} %q_hbm.1) | copy-start | bytes 3145732
  1.9 0.7 %copy-start.1 = (f32[1024]{0:T(1024)S(1)}, f32[1024]{0:T(1024)}, u32[]{:S(2)}) copy-start(f32[1024]{0:T(1024)} %param.9) | copy-start | bytes 12292
